TPU v7x, 256 devices: a whole 4x4x8 slice. The times are simulated.
256 devices in a mesh: stream: 32 (over z, y), item: 8 (over x, core).
Axes of the slice: x: 4, y: 4, z: 8, core: 2. Of those that a mesh axis runs over, the one named last changes fastest.
Arguments:
- event_items: int32 [131072], P('stream'), may hold values from 0 to 262143, as said below
- event_sessions: int32 [131072], P('stream'), may hold values from 0 to 8191, never falling along the last dimension, each value on 1 to 64 neighbouring positions
- sketch_bits: int32 [15, 262144], P(None, 'item'), may hold values from 0 to 262143
Outputs:
- sketch: float32 [128, 256], P('stream')
Inputs may be any that keep to these rules, and one draw needn't show every extreme that they name: `event_items`: item 262144 - 1 occurs at least once.
All inputs are finite; a program needn't handle non-finite values.
Results may differ from a plain program's by a relative error of at most 0.0006.
Values may be sent and summed in bfloat16 or wider, within the bound.
No kernel may reach another device: no remote copies, remote signals or barrier semaphores. Data moves between devices by JAX's collectives and lax.ppermute only.
A program may use at most 128 MiB of HBM per device.

v0:
```python
import math
import jax
import jax.numpy as jnp
from jax import lax
from jax.sharding import PartitionSpec as P

SKETCH = 256
WINDOW = 15
ROWS_DEV = 4


def with_halo(shard, sides, width):
    for axis, dim in sides:
        devices, length = (lax.axis_size(axis), shard.shape[dim])
        up = [(i, (i + 1) % devices) for i in range(devices - 1)]
        down = [(j, i) for i, j in up]
        last = lax.slice_in_dim(shard, length - width, length, axis=dim)
        first = lax.slice_in_dim(shard, 0, width, axis=dim)
        before = lax.ppermute(last, axis, up)
        after = lax.ppermute(first, axis, down)
        shard = jnp.concatenate([before, shard, after], axis=dim)
    return shard


def pointwise(count_block, row_margin, col_margin, pair_total):
    log_ratio = (
        jnp.log(jnp.maximum(count_block, 1.0))
        + jnp.log(pair_total)
        - jnp.log(jnp.maximum(row_margin, 1.0))
        - jnp.log(jnp.maximum(col_margin, 1.0))
    )
    return jnp.where(count_block > 0, jnp.maximum(log_ratio, 0.0), 0.0)


def sign_table(bit_block, sketch_width):
    word_count = bit_block.shape[0]
    spread = jnp.repeat(bit_block, 18, axis=0, total_repeat_length=word_count * 18)[:sketch_width]
    bit_shift = (jnp.arange(sketch_width, dtype=jnp.int32) % 18)[:, None]
    return (2 * jnp.bitwise_and(jnp.right_shift(spread, bit_shift), 1) - 1).astype(jnp.float32)


def slab_pairs(ext_items, ext_sessions, row_items):
    extent = ext_items.shape[0]
    own_count = extent - 2 * WINDOW
    own_sessions = ext_sessions[WINDOW : WINDOW + own_count]
    own_items = ext_items[WINDOW : WINDOW + own_count]
    offset = (
        lax.broadcasted_iota(jnp.int32, (own_count, extent), 1)
        - lax.broadcasted_iota(jnp.int32, (own_count, extent), 0)
        - WINDOW
    )
    nearby = (jnp.abs(offset) <= WINDOW) & (offset != 0)
    same_session = own_sessions[:, None] == ext_sessions[None, :]
    banded = (nearby & same_session).astype(jnp.bfloat16)
    row_hot = (
        own_items[None, :] == lax.broadcasted_iota(jnp.int32, (row_items, own_count), 0)
    ).astype(jnp.bfloat16)
    pair_links = lax.dot_general(
        banded, row_hot, (((0,), (1,)), ((), ())), preferred_element_type=jnp.float32
    )
    weights = jnp.sum(banded, axis=0, dtype=jnp.float32)
    return (pair_links, weights)


def tile_block(links_float, ext_items, first_id, col_count):
    local_ids = ext_items - first_id
    in_band = (local_ids >= 0) & (local_ids < col_count)
    return jax.ops.segment_sum(
        jnp.where(in_band[:, None], links_float, 0.0),
        jnp.where(in_band, local_ids, 0),
        num_segments=col_count,
    )


def band_counts(weights, ext_items, first_id, col_count):
    local_ids = ext_items - first_id
    in_band = (local_ids >= 0) & (local_ids < col_count)
    return jax.ops.segment_sum(
        jnp.where(in_band, weights, 0.0), jnp.where(in_band, local_ids, 0), num_segments=col_count
    )


def local(event_items, event_sessions, sketch_bits):
    slab_count = lax.axis_size("stream")
    band_size = sketch_bits.shape[1]
    owned_cols = band_size // slab_count
    row_items = ROWS_DEV * slab_count
    band_start = lax.axis_index("item") * band_size
    own_start = lax.axis_index("stream") * owned_cols
    total_events = event_items.shape[0] * slab_count
    stacked = jnp.stack([event_items, event_sessions + 1])
    extended = with_halo(stacked, (("stream", 1),), WINDOW)
    pair_links, weights = slab_pairs(extended[0], extended[1], row_items)
    band_margin = band_counts(weights, extended[0], band_start, band_size)
    count_tile = lax.psum_scatter(
        tile_block(
            pair_links, extended[0], band_start, owned_cols * lax.axis_size("stream")
        ).astype(jnp.bfloat16),
        "stream",
        scatter_dimension=0,
        tiled=True,
    ).astype(jnp.float32)
    col_margin = lax.psum_scatter(
        band_margin.astype(jnp.bfloat16), "stream", scatter_dimension=0, tiled=True
    ).astype(jnp.float32)
    row_margin, pair_total = lax.psum(
        (jnp.sum(count_tile, axis=0), jnp.sum(col_margin)), ("stream", "item")
    )
    own_bits = lax.dynamic_slice_in_dim(sketch_bits, own_start, owned_cols, 1)
    sign_rows = sign_table(own_bits, SKETCH)
    positive = pointwise(count_tile, row_margin[None, :], col_margin[:, None], pair_total)
    partial_value = lax.dot_general(
        positive,
        sign_rows,
        (((0,), (1,)), ((), ())),
        precision=lax.Precision.HIGHEST,
        preferred_element_type=jnp.float32,
    )
    summed = lax.psum(partial_value, ("stream", "item"))
    own_rows = lax.dynamic_slice_in_dim(summed, lax.axis_index("stream") * ROWS_DEV, ROWS_DEV, 0)
    return own_rows / math.sqrt(total_events)


def solution(mesh):
    placed = (P("stream"), P("stream"), P(None, "item"))
    return jax.shard_map(
        local, mesh=mesh, in_specs=placed, out_specs=P("stream", None), check_vma=False
    )
```

profile of v0, /device:TPU:8, one launch (start us, length us, event | category | flops | bytes accessed | tf_op | source)
XLA Modules:
  0.0 782.7 jit_solution(2511389435921532583)
XLA Ops:
  6.5 0.0 copy-start
  6.5 0.0 all-reduce.7.cloned.1.call-start
  6.5 0.9 broadcast_add_fusion
  7.4 0.7 fusion.38
  8.2 3.5 collective-permute-start
  11.6 2.4 collective-permute-start.1
  14.0 0.7 pad_add_fusion
  14.8 1.0 iota_compare_fusion.5
  15.8 0.0 collective-permute-done
  15.8 1.3 collective-permute-done.1
  17.1 0.1 concatenate.7
  17.2 0.1 slice_reduce_fusion
  17.3 0.1 and_reduce_fusion
  17.4 0.1 fusion.35
  17.4 34.8 %convert_reduce_fusion = f32[4126]{0:T(1024)S(1)} fusion(s32[4126]{0:T(1024)S(1)} %slice_reduce_fusion, s32[4096]{0:T(1024)S(1)} %broadcast_add_fusion), kind=kLoop, calls=%fused_computation.3 | loop fusion | flops 185896928 | bytes 49392 | tf_op jit(solution)/shard_map/reduce_sum | solution.py:61
  52.3 28.5 %scatter_custom_fusion.1 = f32[32768]{0:T(1024)S(1)} fusion(s32[4126]{0:T(1024)S(1)} %fusion.35, f32[4126]{0:T(1024)S(1)} %broadcast_select_fusion, f32[]{:T(128)} %constant.122.clone.1), kind=kCustom, calls=%fused_computation.41 | custom fusion | flops 4126 | bytes 131076 | tf_op jit(solution)/shard_map/scatter-add | solution.py:78
  80.8 0.6 convert_element_type.26
  81.4 0.0 all-reduce.7.cloned.1.call-update
  81.4 0.2 reduce-scatter.2.cloned.1.call-start
  81.7 35.3 %fusion.7 = f32[4126,128]{1,0:T(8,128)} fusion(s32[4096]{0:T(1024)S(1)} %broadcast_add_fusion, s32[4126]{0:T(1024)S(1)} %slice_reduce_fusion, pred[4126]{0:T(1024)(128)(4,1)S(1)} %and_reduce_fusion, pred[128,4096]{1,0:T(32,128)(4,1)S(1)} %iota_compare_fusion.5), kind=kOutput, calls=%fused_computation.12 | convolution fusion | flops 4462153728 | bytes 2673814 | tf_op jit(solution)/shard_map/dot_general | solution.py:58
  116.9 32.4 %scatter_custom_fusion = f32[32768,128]{1,0:T(8,128)} fusion(s32[4126]{0:T(1024)S(1)} %fusion.35, f32[4126,128]{1,0:T(8,128)} %fusion.7, f32[]{:T(128)} %constant.122.clone.1), kind=kCustom, calls=%fused_computation.10 | custom fusion | flops 528128 | bytes 16777728 | tf_op jit(solution)/shard_map/scatter-add | solution.py:68
  149.4 0.0 copy-start.2
  149.4 0.0 copy-start.1
  149.4 9.0 %convert_element_type.22 = bf16[32768,128]{1,0:T(8,128)(2,1)} convert(f32[32768,128]{1,0:T(8,128)} %scatter_custom_fusion) | non-fusion elementwise | flops 4194304 | bytes 25165824 | tf_op jit(solution)/shard_map/convert_element_type | solution.py:98
  158.3 0.0 reduce-scatter.2.cloned.1.call-update
  158.3 0.0 all-reduce.5.cloned.1.call-start
  158.4 0.0 copy-done.2
  158.4 0.6 dynamic-slice.6
  159.6 0.0 copy-done.1
  159.7 0.0 copy-done
  159.7 1.8 gather_fusion
  161.5 64.1 %all-reduce.7.cloned.1.call-done = bf16[32768]{0:T(1024)(128)(2,1)} async-done(((bf16[32768]{0:T(1024)(128)(2,1)}), bf16[32768]{0:T(1024)(128)(2,1)}) %all-reduce.7.cloned.1.call-update) | async-done | bytes 65552
  225.6 1.3 convert_reduce_fusion.2
  226.9 229.0 %reduce-scatter.2.cloned.1.call-done = bf16[1024,128]{1,0:T(8,128)(2,1)} async-done(((bf16[32768,128]{1,0:T(8,128)(2,1)}), bf16[1024,128]{1,0:T(8,128)(2,1)}) %reduce-scatter.2.cloned.1.call-update) | async-done | bytes 262160 | tf_op jit(solution)/shard_map/reduce_scatter | solution.py:95
  455.9 1.1 convert_reduce_fusion.1
  457.0 74.3 %all-reduce.1 = (f32[128]{0:T(128)S(1)}, f32[]{:T(128)}) all-reduce(f32[128]{0:T(128)S(1)} %convert_reduce_fusion.1, f32[]{:T(128)} %get-tuple-element.19), channel_id=1, replica_groups=mesh['stream'=32,'item'=8] {'stream','item'}, use_global_device_ids=true, to_apply=%region_8.9 | all-reduce | flops 129 | bytes 1032 | tf_op jit(solution)/shard_map/psum | solution.py:106
  532.0 3.0 fusion.14
  535.0 0.0 all-reduce.5.cloned.1.call-update
  535.0 239.9 %all-reduce.5.cloned.1.call-done = f32[128,256]{1,0:T(8,128)} async-done(((f32[128,256]{1,0:T(8,128)}), f32[128,256]{1,0:T(8,128)}) %all-reduce.5.cloned.1.call-update) | async-done | bytes 131088 | tf_op jit(solution)/shard_map/psum | solution.py:119
  774.9 1.3 dynamic-slice_multiply_fusion
  (5 shorter events, 0.0 us)
Async XLA Ops:
  6.5 153.1 %copy-start = (s32[15,32768]{1,0:T(8,128)S(1)}, s32[15,32768]{1,0:T(8,128)}, u32[]{:S(2)}) copy-start(s32[15,32768]{1,0:T(8,128)} %param.7) | copy-start | bytes 5898244
  6.5 219.0 %all-reduce.7.cloned.1.call-start = ((), (), s32[]{:S(2)}) async-start(), calls=%async_computation.3 | async-start | bytes 131072
  8.2 7.6 collective-permute-start
  11.6 5.5 collective-permute-start.1
  81.4 374.5 %reduce-scatter.2.cloned.1.call-start = ((), (), s32[]{:S(2)}) async-start(), calls=%async_computation.1 | async-start | bytes 8650752 | tf_op jit(solution)/shard_map/reduce_scatter | solution.py:95
  149.4 9.0 %copy-start.2 = (u32[256]{0:T(256)S(1)}, u32[256]{0:T(256)}, u32[]{:S(2)}) copy-start(u32[256]{0:T(256)} %constant.143) | copy-start | bytes 3076
  149.4 10.3 %copy-start.1 = (s32[270]{0:T(512)S(1)}, s32[270]{0:T(512)}, u32[]{:S(2)}) copy-start(s32[270]{0:T(512)} %constant.140) | copy-start | bytes 3244
  158.3 616.5 %all-reduce.5.cloned.1.call-start = ((), (), s32[]{:S(2)}) async-start(), calls=%async_computation.2 | async-start | bytes 262144 | tf_op jit(solution)/shard_map/psum | solution.py:119
Sparse Core Ops, SparseCore 0:
  81.5 143.9 all-reduce.6
  229.6 226.2 reduce-scatter.1
  535.1 239.6 all-reduce.4
where the time goes:
time: 783 us
  waiting for transfers between devices  534 us (68%)
  other arithmetic  113 us (14%)
  blocking collectives  74.3 us (9%)
  matrix products  38.3 us (5%)
  between operations  14.6 us (2%)
    psum x1, waiting for transfers between devices, local(): summed = lax.psum(partial_value, ('stream', 'item'))  240 us
    reduce_scatter x1, waiting for transfers between devices, local(): lax.psum_scatter(tile_block(pair_links, extended[0], band_start, owned_co...  229 us
    psum x1, blocking collectives, local(): lax.psum((jnp.sum(count_tile, axis=0), jnp.sum(col_margin)), ('stream', '...  74.3 us
    unnamed x4, waiting for transfers between devices  64.1 us
    dot_general x1, matrix products, slab_pairs(): lax.dot_general(banded, row_hot, (((0,), (1,)), ((), ())), preferred_elem...  35.3 us
    reduce_sum x1, other arithmetic, slab_pairs(): weights = jnp.sum(banded, axis=0, dtype=jnp.float32)  34.8 us
    scatter-add x1, other arithmetic, tile_block(): jax.ops.segment_sum(jnp.where(in_band[:, None], links_float, 0.0), jnp.wh...  32.4 us
    scatter-add x1, other arithmetic, band_counts(): jax.ops.segment_sum(jnp.where(in_band, weights, 0.0), jnp.where(in_band,...  28.5 us
  transfers between devices with their start and end apart: 5, of which 4 were waited for; matrix products, arithmetic and copies ran while one was open for 10% of the time, Pallas kernels for 0%

commit v1 on v0

--- a/solution.py
+++ b/solution.py
@@ -116,7 +116,7 @@
         precision=lax.Precision.HIGHEST,
         preferred_element_type=jnp.float32,
     )
-    summed = lax.psum(partial_value, ("stream", "item"))
+    summed = jnp.sum(lax.all_gather(partial_value, ("stream", "item")), axis=0)
     own_rows = lax.dynamic_slice_in_dim(summed, lax.axis_index("stream") * ROWS_DEV, ROWS_DEV, 0)
     return own_rows / math.sqrt(total_events)
 

time: 783 us -> 706 us (0.902)
  waiting for transfers between devices: 534 us -> 444 us
  other arithmetic: 113 us -> 124 us
    psum x1 -> x0, waiting for transfers between devices: 240 us -> none  [local(): summed = lax.psum(partial_value, ('stream', 'item'))]
    all_gather x0 -> x1, waiting for transfers between devices: none -> 150 us  [local(): summed = jnp.sum(lax.all_gather(partial_value, ('stream', 'item')), axis=0)]
    reduce_sum x0 -> x1, other arithmetic: none -> 12.2 us  [local(): summed = jnp.sum(lax.all_gather(partial_value, ('stream', 'item')), axis=0)]
  transfers between devices with their start and end apart: 5 -> 5, of which waited for: 4 -> 4; matrix products, arithmetic and copies ran while one was open for 10% -> 12% of each run, Pallas kernels for 0% -> 0%
where the time goes in v1:
time: 706 us; the launch traced here: 704 us
  waiting for transfers between devices  444 us (63%)
  other arithmetic  124 us (18%)
  blocking collectives  74.3 us (11%)
  matrix products  38.2 us (5%)
  between operations  14.6 us (2%)
    reduce_scatter x1, waiting for transfers between devices, local(): lax.psum_scatter(tile_block(pair_links, extended[0], band_start, owned_co...  229 us
    all_gather x1, waiting for transfers between devices, local(): summed = jnp.sum(lax.all_gather(partial_value, ('stream', 'item')), axis=0)  150 us
    psum x1, blocking collectives, local(): lax.psum((jnp.sum(count_tile, axis=0), jnp.sum(col_margin)), ('stream', '...  74.3 us
    unnamed x4, waiting for transfers between devices  63.3 us
    dot_general x1, matrix products, slab_pairs(): lax.dot_general(banded, row_hot, (((0,), (1,)), ((), ())), preferred_elem...  35.3 us
    reduce_sum x1, other arithmetic, slab_pairs(): weights = jnp.sum(banded, axis=0, dtype=jnp.float32)  34.8 us
    scatter-add x1, other arithmetic, tile_block(): jax.ops.segment_sum(jnp.where(in_band[:, None], links_float, 0.0), jnp.wh...  32.4 us
    scatter-add x1, other arithmetic, band_counts(): jax.ops.segment_sum(jnp.where(in_band, weights, 0.0), jnp.where(in_band,...  28.5 us
  transfers between devices with their start and end apart: 5, of which 4 were waited for; matrix products, arithmetic and copies ran while one was open for 12% of the time, Pallas kernels for 0%

profile of v1, /device:TPU:8, one launch (start us, length us, event | category | flops | bytes accessed | tf_op | source)
XLA Modules:
  0.0 704.2 jit_solution(7325858636763912590)
XLA Ops:
  6.5 0.0 copy-start
  6.5 0.0 all-reduce.4.cloned.1.call-start
  6.5 0.9 broadcast_add_fusion
  7.4 0.7 fusion.38
  8.2 4.1 collective-permute-start.1
  12.2 1.9 collective-permute-start
  14.2 0.7 pad_add_fusion
  14.9 1.0 iota_compare_fusion.5
  16.0 0.0 collective-permute-done.1
  16.0 1.7 collective-permute-done
  17.7 0.1 concatenate.7
  17.9 0.1 and_reduce_fusion
  17.9 0.1 fusion.35
  18.0 0.1 slice_reduce_fusion
  18.1 34.8 %convert_reduce_fusion = f32[4126]{0:T(1024)S(1)} fusion(s32[4126]{0:T(1024)S(1)} %slice_reduce_fusion, s32[4096]{0:T(1024)S(1)} %broadcast_add_fusion), kind=kLoop, calls=%fused_computation.3 | loop fusion | flops 185896928 | bytes 49392 | tf_op jit(solution)/shard_map/reduce_sum | solution.py:61
  52.9 28.5 %scatter_custom_fusion.1 = f32[32768]{0:T(1024)S(1)} fusion(s32[4126]{0:T(1024)S(1)} %fusion.35, f32[4126]{0:T(1024)S(1)} %broadcast_select_fusion, f32[]{:T(128)} %constant.122.clone.1), kind=kCustom, calls=%fused_computation.41 | custom fusion | flops 4126 | bytes 131076 | tf_op jit(solution)/shard_map/scatter-add | solution.py:78
  81.4 0.6 convert_element_type.26
  82.0 0.0 all-reduce.4.cloned.1.call-update
  82.0 0.2 reduce-scatter.2.cloned.1.call-start
  82.3 35.3 %fusion.7 = f32[4126,128]{1,0:T(8,128)} fusion(s32[4096]{0:T(1024)S(1)} %broadcast_add_fusion, s32[4126]{0:T(1024)S(1)} %slice_reduce_fusion, pred[4126]{0:T(1024)(128)(4,1)S(1)} %and_reduce_fusion, pred[128,4096]{1,0:T(32,128)(4,1)S(1)} %iota_compare_fusion.5), kind=kOutput, calls=%fused_computation.12 | convolution fusion | flops 4462153728 | bytes 2673814 | tf_op jit(solution)/shard_map/dot_general | solution.py:58
  117.6 32.4 %scatter_custom_fusion = f32[32768,128]{1,0:T(8,128)} fusion(s32[4126]{0:T(1024)S(1)} %fusion.35, f32[4126,128]{1,0:T(8,128)} %fusion.7, f32[]{:T(128)} %constant.122.clone.1), kind=kCustom, calls=%fused_computation.10 | custom fusion | flops 528128 | bytes 16777728 | tf_op jit(solution)/shard_map/scatter-add | solution.py:68
  150.0 0.0 copy-start.2
  150.0 0.0 copy-start.1
  150.0 9.0 %convert_element_type.22 = bf16[32768,128]{1,0:T(8,128)(2,1)} convert(f32[32768,128]{1,0:T(8,128)} %scatter_custom_fusion) | non-fusion elementwise | flops 4194304 | bytes 25165824 | tf_op jit(solution)/shard_map/convert_element_type | solution.py:98
  158.9 0.0 reduce-scatter.2.cloned.1.call-update
  159.0 0.0 all-gather.3.cloned.1.call-start
  159.0 0.0 copy-done.2
  159.0 0.6 dynamic-slice.6
  160.3 0.0 copy-done.1
  160.3 0.0 copy-done
  160.3 1.8 gather_fusion
  162.2 63.3 %all-reduce.4.cloned.1.call-done = bf16[32768]{0:T(1024)(128)(2,1)} async-done(((bf16[32768]{0:T(1024)(128)(2,1)}), bf16[32768]{0:T(1024)(128)(2,1)}) %all-reduce.4.cloned.1.call-update) | async-done | bytes 65552
  225.4 1.3 convert_reduce_fusion.2
  226.7 229.0 %reduce-scatter.2.cloned.1.call-done = bf16[1024,128]{1,0:T(8,128)(2,1)} async-done(((bf16[32768,128]{1,0:T(8,128)(2,1)}), bf16[1024,128]{1,0:T(8,128)(2,1)}) %reduce-scatter.2.cloned.1.call-update) | async-done | bytes 262160 | tf_op jit(solution)/shard_map/reduce_scatter | solution.py:95
  455.7 1.1 convert_reduce_fusion.1
  456.8 74.3 %all-reduce.1 = (f32[128]{0:T(128)S(1)}, f32[]{:T(128)}) all-reduce(f32[128]{0:T(128)S(1)} %convert_reduce_fusion.1, f32[]{:T(128)} %get-tuple-element.19), channel_id=1, replica_groups=mesh['stream'=32,'item'=8] {'stream','item'}, use_global_device_ids=true, to_apply=%region_8.9 | all-reduce | flops 129 | bytes 1032 | tf_op jit(solution)/shard_map/psum | solution.py:106
  531.9 2.9 fusion.14
  534.8 0.0 all-gather.3.cloned.1.call-update
  534.9 150.0 %all-gather.3.cloned.1.call-done = f32[32768,256]{1,0:T(8,128)} async-done(((f32[128,256]{1,0:T(8,128)}), f32[32768,256]{1,0:T(8,128)}) %all-gather.3.cloned.1.call-update) | async-done | bytes 33554448 | tf_op jit(solution)/shard_map/all_gather | solution.py:119
  684.9 12.2 %reduce_sum.39 = f32[128,256]{1,0:T(8,128)S(1)} reduce(f32[256,128,256]{2,1,0:T(8,128)} %bitcast.7, f32[]{:T(128)} %constant.122.clone.1), dimensions={0}, to_apply=%region_9.10 | reduce | flops 8355840 | bytes 33685508 | tf_op jit(solution)/shard_map/reduce_sum | solution.py:119
  697.1 0.6 dynamic-slice_multiply_fusion
  (5 shorter events, 0.0 us)
Async XLA Ops:
  6.5 153.8 %copy-start = (s32[15,32768]{1,0:T(8,128)S(1)}, s32[15,32768]{1,0:T(8,128)}, u32[]{:S(2)}) copy-start(s32[15,32768]{1,0:T(8,128)} %param.7) | copy-start | bytes 5898244
  6.5 218.9 %all-reduce.4.cloned.1.call-start = ((), (), s32[]{:S(2)}) async-start(), calls=%async_computation.3 | async-start | bytes 131072
  8.2 7.8 %collective-permute-start.1 = (s32[2,15]{1,0:T(2,128)S(1)}, s32[2,15]{1,0:T(2,128)S(1)}, u32[]{:S(2)}, u32[]{:S(2)}) collective-permute-start(s32[2,15]{1,0:T(2,128)S(1)} %get-tuple-element.21), channel_id=1, source_target_pairs={{8,0},{16,8},{24,16},{32,24},{40,32},{48,40},{56,48},{64,56},{72,6... | collective-permute-start | bytes 368 | tf_op jit(solution)/shard_map/ppermute | solution.py:20
  12.2 5.5 collective-permute-start
  82.0 373.7 %reduce-scatter.2.cloned.1.call-start = ((), (), s32[]{:S(2)}) async-start(), calls=%async_computation.1 | async-start | bytes 8650752 | tf_op jit(solution)/shard_map/reduce_scatter | solution.py:95
  150.0 9.1 %copy-start.2 = (u32[256]{0:T(256)S(1)}, u32[256]{0:T(256)}, u32[]{:S(2)}) copy-start(u32[256]{0:T(256)} %constant.143) | copy-start | bytes 3076
  150.0 10.3 %copy-start.1 = (s32[270]{0:T(512)S(1)}, s32[270]{0:T(512)}, u32[]{:S(2)}) copy-start(s32[270]{0:T(512)} %constant.140) | copy-start | bytes 3244
  159.0 525.9 %all-gather.3.cloned.1.call-start = ((), (), s32[]{:S(2)}) async-start(), calls=%async_computation.2 | async-start | bytes 33685504 | tf_op jit(solution)/shard_map/all_gather | solution.py:119
Sparse Core Ops, SparseCore 0:
  82.2 143.2 all-reduce.3
  229.4 226.2 reduce-scatter.1
  535.0 149.8 all-gather.2
